TPU v7x, 32 devices: a whole 2x2x4 slice. The times are simulated.
32 devices in a mesh: row: 8 (over y, x, core), col: 4 (over z).
Axes of the slice: x: 2, y: 2, z: 4, core: 2. Of those that a mesh axis runs over, the one named last changes fastest.
Arguments:
- shear_stress: float32 [512, 16384], P(None, ('row', 'col')), may hold values from -3.5 to 3.5
- state_var: float32 [512, 16384], P(None, ('row', 'col')), may hold values from -0.4 to 0.4
- a_param: float32 [16384], P(('row', 'col')), may hold values from 0.7 to 1.4
- rate_param: float32 [16384], P(('row', 'col')), may hold values from 0.1 to 0.5
- loading: float32 [16384], P(('row', 'col')), may hold values from 0.1 to 1
- dense_tiles: bfloat16 [16384, 16384], P('row', 'col'), may hold values from -0.046875 to 0.046875
- left_factor: bfloat16 [512, 16384], P('col', 'row'), may hold values from -0.75 to 0.75
- right_factor: bfloat16 [512, 16384], P('row', 'col'), may hold values from -0.046875 to 0.046875
- admissible: int32 [8, 8], replicated, may hold values from 0 to 1, as said below
- tile_ranks: int32 [8, 8], replicated, may hold values from 16 to 64
Outputs:
- shear_next: float32 [512, 16384], P(None, ('row', 'col'))
- state_next: float32 [512, 16384], P(None, ('row', 'col'))
Inputs may be any that keep to these rules, and one draw needn't show every extreme that they name: `admissible`: tiles on the diagonal and next to it are always dense; elsewhere a tile is dense or low-rank at random.
All inputs are finite; a program needn't handle non-finite values.
Results may differ from a plain program's by a relative error of at most 0.0024.
Values may be sent and summed in bfloat16 or wider, within the bound.
A program may use at most 128 MiB of HBM per device.

v0:
```python
import functools
import math

import jax
import jax.numpy as jnp
from jax import lax
from jax.experimental import pallas as pl
from jax.experimental.pallas import tpu as pltpu
from jax.sharding import PartitionSpec as P

TILE = 2048
RANK = 64
GROUP = 16
LAG = 4
LN2 = math.log(2.0)
MESH = pl.DeviceIdType.MESH
F32 = jnp.float32
BF16 = jnp.bfloat16


def kernel(
    rows,
    cols,
    shear_ref,
    state_ref,
    a_ref,
    rate_ref,
    load_ref,
    dense_ref,
    left_ref,
    right_ref,
    adm_ref,
    rank_ref,
    shear_out,
    state_out,
    weights,
    gathered,
    vsend,
    staged,
    psend,
    precv,
    own,
    k_shear,
    k_state,
    dense_sem,
    st_send,
    st_recv,
    p1_send,
    p1_recv,
    p2_send,
    fwd_send,
    p2_recv,
    rs_send,
    rs_recv,
):
    scenarios, piece = shear_ref.shape
    chunk = rows * GROUP
    chunks = scenarios // chunk
    gap = max(0, LAG - chunks)
    half = rows // 2
    per = rows // cols
    r = lax.axis_index("row")
    c = lax.axis_index("col")
    mine = c * per
    sib = r + 1 - 2 * (r % 2)
    targets, sources = weights.shape
    across = sources // TILE
    down = targets // TILE

    dense_copy = pltpu.make_async_copy(dense_ref, weights, dense_sem)

    def scen(q):
        return pl.ds(pl.multiple_of(q * chunk, chunk), chunk)

    def group_of(u, g):
        return gathered.at[u, pl.ds(pl.multiple_of(g * GROUP, GROUP), GROUP), :]

    def part_of(u, g):
        return vsend.at[u, pl.ds(pl.multiple_of(g * GROUP, GROUP), GROUP), :]

    def st_copy(u, j):
        return pltpu.make_async_remote_copy(
            src_ref=part_of(u, j),
            dst_ref=staged.at[u, r],
            send_sem=st_send.at[u, j],
            recv_sem=st_recv.at[u],
            device_id=(j, c),
            device_id_type=MESH,
        )

    def place(u, source):
        slot = (source % per) * cols + c
        return gathered.at[
            u,
            pl.ds(pl.multiple_of(r * GROUP, GROUP), GROUP),
            pl.ds(pl.multiple_of(slot * piece, piece), piece),
        ]

    def p1_copy(u, source):
        return pltpu.make_async_remote_copy(
            src_ref=staged.at[u, source],
            dst_ref=place(u, source),
            send_sem=p1_send.at[u, source],
            recv_sem=p1_recv.at[u],
            device_id=(r, source // per),
            device_id_type=MESH,
        )

    def group_copy(u, g, send_sem, row_to):
        return pltpu.make_async_remote_copy(
            src_ref=group_of(u, g),
            dst_ref=group_of(u, g),
            send_sem=send_sem,
            recv_sem=p2_recv.at[u, g],
            device_id=(row_to, c),
            device_id_type=MESH,
        )

    def rs_copy(u, z):
        return pltpu.make_async_remote_copy(
            src_ref=psend.at[u, z],
            dst_ref=precv.at[u, c],
            send_sem=rs_send.at[u, z],
            recv_sem=rs_recv.at[u, c],
            device_id=(r, z),
            device_id_type=MESH,
        )

    def rs_arrival(u, z):
        return pltpu.make_async_remote_copy(
            src_ref=psend.at[u, z],
            dst_ref=precv.at[u, z],
            send_sem=rs_send.at[u, z],
            recv_sem=rs_recv.at[u, z],
            device_id=(r, z),
            device_id_type=MESH,
        )

    def velocity(shear_now, state_now):
        x = shear_now / a_ref[...]
        fade = jnp.exp(-state_now)
        v = (jnp.exp(x - LN2) - jnp.exp(-x - LN2)) * fade
        return v, rate_ref[...] * (fade - jnp.abs(v))

    def send_slip(u):
        def one(i, _):
            st_copy(u, (r + 1 + i) % rows).start()
            return 0

        lax.fori_loop(0, rows - 1, one, 0)
        pltpu.make_async_copy(part_of(u, r), staged.at[u, r], st_recv.at[u]).start()

    def relay(u):
        pltpu.make_async_copy(staged.at[u], staged.at[u], st_recv.at[u]).wait()

        def one(i, _):
            p1_copy(u, (mine + per + i) % rows).start()
            return 0

        lax.fori_loop(0, rows - per, one, 0)

        def stay(i, _):
            pltpu.make_async_copy(
                staged.at[u, mine + i], place(u, mine + i), p1_recv.at[u]
            ).start()
            return 0

        lax.fori_loop(0, per, stay, 0)

    def first_slip(q, _):
        v, ks = velocity(shear_ref[scen(q), :], state_ref[scen(q), :])
        vsend[q] = v.astype(BF16)
        k_state[scen(q), :] = ks
        send_slip(q)
        return 0

    def spread(u):
        pltpu.make_async_copy(group_of(u, r), group_of(u, r), p1_recv.at[u]).wait()
        group_copy(u, r, p2_send.at[u, half - 1], sib).start()

        def one(i, _):
            group_copy(u, r, p2_send.at[u, i], (r + 2 * (i + 1)) % rows).start()
            return 0

        lax.fori_loop(0, half - 1, one, 0)

    def forward(u):
        def one(i, _):
            g = (r + 2 * (i + 1)) % rows
            group_copy(u, g, fwd_send.at[u, i], sib).wait_recv()
            group_copy(u, g, fwd_send.at[u, i], sib).start()
            return 0

        lax.fori_loop(0, half - 1, one, 0)

    def multiply(u):
        def arrive(i, _):
            group_copy(u, (sib + 2 * i) % rows, p1_send.at[u, 0], sib).wait_recv()
            return 0

        lax.fori_loop(0, half, arrive, 0)

        def one(i, _):
            z = (c + 1 + i) % cols
            part = lax.dot_general(
                gathered[u],
                weights[pl.ds(pl.multiple_of(z * piece, piece), piece), :],
                (((1,), (1,)), ((), ())),
                preferred_element_type=F32,
            )

            @pl.when(i < cols - 1)
            def _():
                psend[u, z] = part.astype(BF16)
                rs_copy(u, z).start()

            @pl.when(i == cols - 1)
            def _():
                own[u] = part

            return 0

        lax.fori_loop(0, cols, one, 0)

    def finish(u):
        def one(i, _):
            z = (c + 1 + i) % cols
            rs_arrival(u, z).wait_recv()
            own[u] = own[u] + precv[u, z].astype(F32)
            return 0

        lax.fori_loop(0, cols - 1, one, 0)

        @pl.when(u < chunks)
        def _():
            here = scen(u)
            ks = load_ref[...] - own[u]
            k_shear[here, :] = ks
            k1 = k_state[here, :]
            state = state_ref[here, :]
            v, k2 = velocity(shear_ref[here, :] + 0.5 * ks, state + 0.5 * k1)
            vsend[u + chunks] = v.astype(BF16)
            send_slip(u + chunks)
            state_out[here, :] = state + 0.25 * (k1 + k2)

        @pl.when(u >= chunks)
        def _():
            here = scen(u - chunks)
            ks = load_ref[...] - own[u]
            shear_out[here, :] = shear_ref[here, :] + 0.25 * (k_shear[here, :] + ks)

    build_rows = 256
    builds = targets // build_rows
    build_cols = 512

    def build(b, _):
        start = pl.multiple_of(b * build_rows, build_rows)
        here = pl.ds(start, build_rows)
        td = (b * build_rows) // TILE
        for k in range(across):
            dense = adm_ref[r * down + td, c * across + k]
            rank = rank_ref[r * down + td, c * across + k]
            left = left_ref[k * RANK : (k + 1) * RANK, here]
            keep = lax.broadcasted_iota(jnp.int32, (RANK, build_rows), 0) < rank
            left = jnp.where(keep, left.astype(F32), 0.0)
            left = jnp.transpose(left).astype(BF16)
            for s in range(TILE // build_cols):
                span = slice(k * TILE + s * build_cols, k * TILE + (s + 1) * build_cols)
                right = right_ref[pl.ds(pl.multiple_of(td * RANK, RANK), RANK), span]
                term = jnp.dot(left, right, preferred_element_type=F32)
                is_dense = jnp.full(term.shape, dense, jnp.int32) == 1
                weights[here, span] = jnp.where(
                    is_dense, weights[here, span].astype(F32), term
                ).astype(BF16)
        return 0

    dense_copy.start()
    lax.fori_loop(0, chunks, first_slip, 0)

    def first_relay(q, _):
        relay(q)
        return 0

    lax.fori_loop(0, chunks, first_relay, 0)

    def at_slot(sigma, body):
        valid = ((sigma >= 0) & (sigma < chunks)) | (
            (sigma >= chunks + gap) & (sigma < 2 * chunks + gap)
        )
        u = jnp.where(sigma < chunks, sigma, sigma - gap)

        @pl.when(valid)
        def _():
            body(u)

    def step(t, _):
        at_slot(t - 2, multiply)

        @pl.when((t >= chunks + gap) & (t < 2 * chunks + gap))
        def _():
            relay(t - gap)

        at_slot(t - 1, forward)
        at_slot(t, spread)

        @pl.when(t == 0)
        def _():
            dense_copy.wait()

        @pl.when(t < 2)
        def _():
            lax.fori_loop(t * builds // 2, (t + 1) * builds // 2, build, 0)

        at_slot(t - 3, finish)
        return 0

    lax.fori_loop(0, 2 * chunks + gap + 3, step, 0)

    def drain(u, _):
        def st(i, _):
            st_copy(u, (r + 1 + i) % rows).wait_send()
            return 0

        lax.fori_loop(0, rows - 1, st, 0)

        def p1(i, _):
            p1_copy(u, (mine + per + i) % rows).wait_send()
            return 0

        lax.fori_loop(0, rows - per, p1, 0)

        def p2(i, _):
            group_copy(u, r, p2_send.at[u, i], sib).wait_send()
            return 0

        lax.fori_loop(0, half, p2, 0)

        def fwd(i, _):
            group_copy(u, r, fwd_send.at[u, i], sib).wait_send()
            return 0

        lax.fori_loop(0, half - 1, fwd, 0)

        def rs(i, _):
            rs_copy(u, (c + 1 + i) % cols).wait_send()
            return 0

        lax.fori_loop(0, cols - 1, rs, 0)
        return 0

    lax.fori_loop(0, 2 * chunks, drain, 0)


def solution(mesh):
    rows, cols = mesh.shape["row"], mesh.shape["col"]

    def on_device(
        shear, state, a_param, rate, loading, dense, left, right, admissible, ranks
    ):
        scenarios, piece = shear.shape
        chunk = rows * GROUP
        units = 2 * (scenarios // chunk)
        vmem = pl.BlockSpec(memory_space=pltpu.VMEM)
        smem = pl.BlockSpec(memory_space=pltpu.SMEM)
        hbm = pl.BlockSpec(memory_space=pl.ANY)
        dma = pltpu.SemaphoreType.DMA
        return pl.pallas_call(
            functools.partial(kernel, rows, cols),
            out_shape=(
                jax.ShapeDtypeStruct(shear.shape, F32),
                jax.ShapeDtypeStruct(shear.shape, F32),
            ),
            in_specs=[vmem] * 5 + [hbm, vmem, vmem, smem, smem],
            out_specs=(vmem, vmem),
            scratch_shapes=[
                pltpu.VMEM(dense.shape, BF16),
                pltpu.VMEM((units, chunk, dense.shape[1]), BF16),
                pltpu.VMEM((units, chunk, piece), BF16),
                pltpu.VMEM((units, rows, GROUP, piece), BF16),
                pltpu.VMEM((units, cols, chunk, piece), BF16),
                pltpu.VMEM((units, cols, chunk, piece), BF16),
                pltpu.VMEM((units, chunk, piece), F32),
                pltpu.VMEM(shear.shape, F32),
                pltpu.VMEM(shear.shape, F32),
                dma,
                dma((units, rows)),
                dma((units,)),
                dma((units, rows)),
                dma((units,)),
                dma((units, rows // 2)),
                dma((units, rows // 2)),
                dma((units, rows)),
                dma((units, cols)),
                dma((units, cols)),
            ],
            compiler_params=pltpu.CompilerParams(
                has_side_effects=True, vmem_limit_bytes=62 * 1024 * 1024
            ),
        )(
            shear,
            state,
            a_param[None, :],
            rate[None, :],
            loading[None, :],
            dense,
            left,
            right,
            admissible,
            ranks,
        )

    wide = P(None, ("row", "col"))
    line = P(("row", "col"))
    placed = (
        wide,
        wide,
        line,
        line,
        line,
        P("row", "col"),
        P("col", "row"),
        P("row", "col"),
        P(),
        P(),
    )
    return jax.shard_map(
        on_device, mesh=mesh, in_specs=placed, out_specs=(wide, wide), check_vma=False
    )
```

profile of v0, /device:TPU:0, one launch (start us, length us, event | category | flops | bytes accessed | tf_op | source)
XLA Modules:
  0.0 158.4 jit_solution(17296030060554413027)
XLA Ops:
  0.6 153.2 %shard_map.113 = (f32[512,512]{1,0:T(8,128)}, f32[512,512]{1,0:T(8,128)}) custom-call(f32[512,512]{1,0:T(8,128)} %shear_ref.1, f32[512,512]{1,0:T(8,128)} %state_ref.1, f32[1,512]{1,0:T(1,128)} %bitcast.3, f32[1,512]{1,0:T(1,128)} %bitcast.4, f32[1,512]{1,0:T(1,128)} %bitcast.5, bf16[2048,4096]{1,0:T(8,128)(2,1)} %dense_ref.1, bf16[128,2048]{1,0:T(8,128)(2,1)} %left_ref.1, ...), custom_call_target="tpu_custom_call" | custom-call | tf_op jit(solution)/shard_map/pallas_call | solution.py:367
  153.9 2.3 %copy.14 = f32[512,512]{1,0:T(8,128)} copy(f32[512,512]{1,0:T(8,128)} %get-tuple-element.4) | data formatting | bytes 2097152
  156.1 2.3 %copy.15 = f32[512,512]{1,0:T(8,128)} copy(f32[512,512]{1,0:T(8,128)} %get-tuple-element.5) | data formatting | bytes 2097152
where the time goes:
time: 159 us; the launch traced here: 158 us
  Pallas kernels  153 us (96%)
  local copies, waits for them, and re-layouts  4.52 us (3%)
    pallas_call x1, Pallas kernels, on_device(): pl.pallas_call(functools.partial(kernel, rows, cols), out_shape=(jax.Shap...  153 us
    unnamed x2, local copies, waits for them, and re-layouts  4.52 us

commit v1 on v0

v1 whole, which is shorter than its diff:
```python
import functools
import math

import jax
import jax.numpy as jnp
from jax import lax
from jax.experimental import pallas as pl
from jax.experimental.pallas import tpu as pltpu
from jax.sharding import PartitionSpec as P

TILE = 2048
RANK = 64
GROUP = 16
LAG = 4
LN2 = math.log(2.0)
MESH = pl.DeviceIdType.MESH
F32 = jnp.float32
BF16 = jnp.bfloat16


def kernel(
    rows,
    cols,
    shear_hbm,
    state_hbm,
    a_ref,
    rate_ref,
    load_ref,
    dense_ref,
    left_ref,
    right_ref,
    adm_ref,
    rank_ref,
    shear_out,
    state_out,
    weights,
    gathered,
    vsend,
    staged,
    partial,
    psend,
    precv,
    own,
    shear,
    state,
    k_shear,
    k_state,
    dense_sem,
    in_sem,
    out_sem,
    st_send,
    st_recv,
    p1_send,
    p1_recv,
    p2_send,
    p2_recv,
    sib_send,
    sib_recv,
    rs_send,
    rs_recv,
):
    scenarios, piece = shear.shape
    chunk = rows * GROUP
    chunks = scenarios // chunk
    units = 2 * chunks
    half = rows // 2
    per = rows // cols
    slots = partial.shape[0]
    r = lax.axis_index("row")
    c = lax.axis_index("col")
    mine = c * per
    sib = r + 1 - 2 * (r % 2)
    targets, sources = weights.shape
    across = sources // TILE
    build_rows = 256
    builds = targets // build_rows
    build_cols = 512
    low = c < cols // 2
    middle = (c > 0) & (c < cols - 1)

    def scen(q):
        return pl.ds(pl.multiple_of(q * chunk, chunk), chunk)

    def shear_in(q):
        return pltpu.make_async_copy(
            shear_hbm.at[scen(q), :], shear.at[scen(q), :], in_sem.at[0, q]
        )

    def state_in(q):
        return pltpu.make_async_copy(
            state_hbm.at[scen(q), :], state.at[scen(q), :], in_sem.at[1, q]
        )

    def shear_store(q):
        return pltpu.make_async_copy(
            shear.at[scen(q), :], shear_out.at[scen(q), :], out_sem.at[0, q]
        )

    def state_store(q):
        return pltpu.make_async_copy(
            state.at[scen(q), :], state_out.at[scen(q), :], out_sem.at[1, q]
        )

    def dense_in(b):
        span = pl.ds(pl.multiple_of(b * build_rows, build_rows), build_rows)
        return pltpu.make_async_copy(
            dense_ref.at[span, :], weights.at[span, :], dense_sem.at[b]
        )

    def group_of(u, g):
        return gathered.at[u, pl.ds(pl.multiple_of(g * GROUP, GROUP), GROUP), :]

    def part_of(u, g):
        return vsend.at[u, pl.ds(pl.multiple_of(g * GROUP, GROUP), GROUP), :]

    def st_copy(u, j):
        return pltpu.make_async_remote_copy(
            src_ref=part_of(u, j),
            dst_ref=staged.at[u, r],
            send_sem=st_send.at[u],
            recv_sem=st_recv.at[u],
            device_id=(j, c),
            device_id_type=MESH,
        )

    def place(u, source):
        slot = (source % per) * cols + c
        return gathered.at[
            u,
            pl.ds(pl.multiple_of(r * GROUP, GROUP), GROUP),
            pl.ds(pl.multiple_of(slot * piece, piece), piece),
        ]

    def p1_copy(u, source):
        return pltpu.make_async_remote_copy(
            src_ref=staged.at[u, source],
            dst_ref=place(u, source),
            send_sem=p1_send.at[u],
            recv_sem=p1_recv.at[u],
            device_id=(r, source // per),
            device_id_type=MESH,
        )

    def plane_copy(u, g, row_to):
        return pltpu.make_async_remote_copy(
            src_ref=group_of(u, g),
            dst_ref=group_of(u, g),
            send_sem=p2_send.at[u],
            recv_sem=p2_recv.at[u, g],
            device_id=(row_to, c),
            device_id_type=MESH,
        )

    def sib_copy(u, g):
        return pltpu.make_async_remote_copy(
            src_ref=group_of(u, g),
            dst_ref=group_of(u, g),
            send_sem=sib_send.at[u],
            recv_sem=sib_recv.at[u],
            device_id=(sib, c),
            device_id_type=MESH,
        )

    def rs_copy(u, d, up):
        to = jnp.where(up, c + 1, c - 1)
        slot = jnp.where(up | (d < to), d, cols)
        return pltpu.make_async_remote_copy(
            src_ref=psend.at[u, d],
            dst_ref=precv.at[u, slot],
            send_sem=rs_send.at[u],
            recv_sem=rs_recv.at[u, slot],
            device_id=(r, to),
            device_id_type=MESH,
        )

    def rs_arrival(u, slot):
        return pltpu.make_async_copy(
            precv.at[u, slot], precv.at[u, slot], rs_recv.at[u, slot]
        )

    inv_a = 1.0 / a_ref[...]

    def velocity(shear_now, state_now):
        x = shear_now * inv_a
        fade = jnp.exp(-state_now)
        v = (jnp.exp(x - LN2) - jnp.exp(-x - LN2)) * fade
        return v, rate_ref[...] * (fade - jnp.abs(v))

    def send_slip(u):
        def one(i, _):
            st_copy(u, (r + 1 + i) % rows).start()
            return 0

        lax.fori_loop(0, rows - 1, one, 0)
        pltpu.make_async_copy(part_of(u, r), staged.at[u, r], st_recv.at[u]).start()

    def relay(u):
        pltpu.make_async_copy(staged.at[u], staged.at[u], st_recv.at[u]).wait()

        def one(i, _):
            p1_copy(u, (mine + per + i) % rows).start()
            return 0

        lax.fori_loop(0, rows - per, one, 0)

        def stay(i, _):
            pltpu.make_async_copy(
                staged.at[u, mine + i], place(u, mine + i), p1_recv.at[u]
            ).start()
            return 0

        lax.fori_loop(0, per, stay, 0)

    def first_slip(q, _):
        shear_in(q).wait()
        state_in(q).wait()
        v, ks = velocity(shear[scen(q), :], state[scen(q), :])
        vsend[q] = v.astype(BF16)
        k_state[scen(q), :] = ks
        return 0

    def spread(u):
        pltpu.make_async_copy(group_of(u, r), group_of(u, r), p1_recv.at[u]).wait()

        def one(i, _):
            plane_copy(u, r, (r + 2 * (i + 1)) % rows).start()
            return 0

        lax.fori_loop(0, half - 1, one, 0)
        sib_copy(u, r).start()

    def forward(u):
        def one(i, _):
            g = (r + 2 * (i + 1)) % rows
            plane_copy(u, g, sib).wait_recv()
            sib_copy(u, g).start()
            return 0

        lax.fori_loop(0, half - 1, one, 0)

    def gather_end(u):
        span = pl.ds(0, half * GROUP)
        pltpu.make_async_copy(
            gathered.at[u, span, :], gathered.at[u, span, :], sib_recv.at[u]
        ).wait()

    def multiply(u, i):
        d = jnp.where(low, c + cols - 1 - i, c + 1 + i) % cols
        part = lax.dot_general(
            gathered[u],
            weights[pl.ds(pl.multiple_of(d * piece, piece), piece), :],
            (((1,), (1,)), ((), ())),
            preferred_element_type=F32,
        )

        @pl.when(d == c)
        def _():
            own[u % slots] = part

        @pl.when((d != c) & middle)
        def _():
            partial[u % slots, d] = part

        @pl.when((d != c) & jnp.logical_not(middle))
        def _():
            psend[u, d] = part.astype(BF16)
            rs_copy(u, d, c == 0).start()

    def hop(u, up):
        def one(i, _):
            d = jnp.where(up, cols - 1 - i, i)
            rs_arrival(u, d).wait()
            psend[u, d] = (partial[u % slots, d] + precv[u, d].astype(F32)).astype(BF16)
            rs_copy(u, d, up).start()
            return 0

        @pl.when(middle)
        def _():
            lax.fori_loop(0, jnp.where(up, cols - 1 - c, c), one, 0)

    def finish(u):
        @pl.when(c > 0)
        def _():
            rs_arrival(u, c).wait()
            own[u % slots] = own[u % slots] + precv[u, c].astype(F32)

        @pl.when(c < cols - 1)
        def _():
            rs_arrival(u, cols).wait()
            own[u % slots] = own[u % slots] + precv[u, cols].astype(F32)

        @pl.when(u < chunks)
        def _():
            here = scen(u)
            ks = load_ref[...] - own[u % slots]
            k_shear[here, :] = ks
            k1 = k_state[here, :]
            old = state[here, :]
            v, k2 = velocity(shear[here, :] + 0.5 * ks, old + 0.5 * k1)
            vsend[u + chunks] = v.astype(BF16)
            send_slip(u + chunks)
            state[here, :] = old + 0.25 * (k1 + k2)
            state_store(u).start()

        @pl.when(u >= chunks)
        def _():
            here = scen(u - chunks)
            ks = load_ref[...] - own[u % slots]
            shear[here, :] = shear[here, :] + 0.25 * (k_shear[here, :] + ks)
            shear_store(u - chunks).start()

    def build_order(i):
        if builds % cols:
            return i
        each = builds // cols
        d = jnp.where(low, c + cols - 1 - i // each, c + 1 + i // each) % cols
        return d * each + i % each

    def build(i, _):
        b = build_order(i)
        dense_in(b).wait()
        here = pl.ds(pl.multiple_of(b * build_rows, build_rows), build_rows)
        down = targets // TILE
        td = (b * build_rows) // TILE
        for k in range(across):
            dense = adm_ref[r * down + td, c * across + k]
            rank = rank_ref[r * down + td, c * across + k]
            kept = jnp.where(dense == 1, 0, rank)
            left = left_ref[k * RANK : (k + 1) * RANK, here]
            keep = lax.broadcasted_iota(jnp.int32, (RANK, build_rows), 0) < kept
            left = jnp.where(keep, left.astype(F32), 0.0)
            left = jnp.transpose(left).astype(BF16)
            scale = jnp.where(dense == 1, 1.0, 0.0).astype(F32)
            scale = jnp.full((build_rows, build_cols), scale, F32).astype(BF16)
            for s in range(TILE // build_cols):
                span = slice(k * TILE + s * build_cols, k * TILE + (s + 1) * build_cols)
                right = right_ref[pl.ds(pl.multiple_of(td * RANK, RANK), RANK), span]
                term = jnp.dot(left, right, preferred_element_type=F32).astype(BF16)
                weights[here, span] = weights[here, span] * scale + term
        return 0

    def drain(u):
        def sent(ref, sem):
            pltpu.make_async_copy(ref, ref, sem).wait()

        sent(vsend.at[u, pl.ds(0, (rows - 1) * GROUP), :], st_send.at[u])
        sent(staged.at[u, pl.ds(0, rows - per)], p1_send.at[u])
        sent(gathered.at[u, pl.ds(0, (half - 1) * GROUP), :], p2_send.at[u])
        sent(gathered.at[u, pl.ds(0, half * GROUP), :], sib_send.at[u])
        sent(psend.at[u, pl.ds(0, cols - 1)], rs_send.at[u])

    barrier = pltpu.get_barrier_semaphore()

    def greet_row(i, _):
        pl.semaphore_signal(
            barrier, inc=1, device_id=((r + 1 + i) % rows, c), device_id_type=MESH
        )
        return 0

    def greet_col(i, _):
        pl.semaphore_signal(
            barrier, inc=1, device_id=(r, (c + 1 + i) % cols), device_id_type=MESH
        )
        return 0

    lax.fori_loop(0, rows - 1, greet_row, 0)
    lax.fori_loop(0, cols - 1, greet_col, 0)

    def fetch(q, _):
        shear_in(q).start()
        state_in(q).start()
        return 0

    lax.fori_loop(0, chunks, fetch, 0)

    def fetch_dense(i, _):
        dense_in(build_order(i)).start()
        return 0

    lax.fori_loop(0, builds, fetch_dense, 0)
    lax.fori_loop(0, chunks, first_slip, 0)
    cuts = [builds * k // 8 for k in (0, 2, 4, 6, 8)]
    lax.fori_loop(cuts[0], cuts[1], build, 0)
    pl.semaphore_wait(barrier, rows + cols - 2)

    def first_send(q, _):
        send_slip(q)
        return 0

    lax.fori_loop(0, chunks, first_send, 0)
    lax.fori_loop(cuts[1], cuts[2], build, 0)

    def first_relay(q, _):
        relay(q)
        return 0

    lax.fori_loop(0, chunks, first_relay, 0)
    lax.fori_loop(cuts[2], cuts[3], build, 0)
    spread(0)
    spread(1)
    lax.fori_loop(cuts[3], cuts[4], build, 0)
    forward(0)

    gap = max(0, LAG - chunks)

    def at_slot(sigma, body, also=True):
        valid = ((sigma >= 0) & (sigma < chunks)) | (
            (sigma >= chunks + gap) & (sigma < units + gap)
        )

        @pl.when(valid & also)
        def _():
            body(jnp.where(sigma < chunks, sigma, sigma - gap))

    def step(t, _):
        at_slot(t - 1, lambda u: hop(u, low))
        early = t + 2 < chunks
        at_slot(jnp.where(early, t + 2, t + 1), spread, early | (t + 1 >= chunks))
        at_slot(t - 2, finish)
        at_slot(t, gather_end)

        def one(i, _):
            at_slot(t, lambda u: multiply(u, i))
            at_slot(t + 2, relay, (i == 0) & (t + 2 >= chunks))
            at_slot(t - 1, lambda u: hop(u, jnp.logical_not(low)), i == 1)
            return 0

        lax.fori_loop(0, cols, one, 0)
        at_slot(t + 1, forward)
        at_slot(t - 4, drain)
        return 0

    lax.fori_loop(0, units + gap + 2, step, 0)

    def last(u, _):
        drain(u)
        return 0

    lax.fori_loop(units - 2, units, last, 0)

    def stored(q, _):
        shear_store(q).wait()
        state_store(q).wait()
        return 0

    lax.fori_loop(0, chunks, stored, 0)


def solution(mesh):
    rows, cols = mesh.shape["row"], mesh.shape["col"]

    def on_device(
        shear, state, a_param, rate, loading, dense, left, right, admissible, ranks
    ):
        scenarios, piece = shear.shape
        chunk = rows * GROUP
        chunks = scenarios // chunk
        units = 2 * chunks
        slots = min(units, 4)
        vmem = pl.BlockSpec(memory_space=pltpu.VMEM)
        smem = pl.BlockSpec(memory_space=pltpu.SMEM)
        hbm = pl.BlockSpec(memory_space=pl.ANY)
        dma = pltpu.SemaphoreType.DMA
        return pl.pallas_call(
            functools.partial(kernel, rows, cols),
            out_shape=(
                jax.ShapeDtypeStruct(shear.shape, F32),
                jax.ShapeDtypeStruct(shear.shape, F32),
            ),
            in_specs=[hbm] * 2 + [vmem] * 3 + [hbm, vmem, vmem, smem, smem],
            out_specs=(hbm, hbm),
            scratch_shapes=[
                pltpu.VMEM(dense.shape, BF16),
                pltpu.VMEM((units, chunk, dense.shape[1]), BF16),
                pltpu.VMEM((units, chunk, piece), BF16),
                pltpu.VMEM((units, rows, GROUP, piece), BF16),
                pltpu.VMEM((slots, cols, chunk, piece), F32),
                pltpu.VMEM((units, cols, chunk, piece), BF16),
                pltpu.VMEM((units, cols + 1, chunk, piece), BF16),
                pltpu.VMEM((slots, chunk, piece), F32),
                pltpu.VMEM(shear.shape, F32),
                pltpu.VMEM(shear.shape, F32),
                pltpu.VMEM(shear.shape, F32),
                pltpu.VMEM(shear.shape, F32),
                dma((dense.shape[0] // 256,)),
                dma((2, chunks)),
                dma((2, chunks)),
                dma((units,)),
                dma((units,)),
                dma((units,)),
                dma((units,)),
                dma((units,)),
                dma((units, rows)),
                dma((units,)),
                dma((units,)),
                dma((units,)),
                dma((units, cols + 1)),
            ],
            compiler_params=pltpu.CompilerParams(
                collective_id=0,
                has_side_effects=True,
                vmem_limit_bytes=62 * 1024 * 1024,
            ),
        )(
            shear,
            state,
            a_param[None, :],
            rate[None, :],
            loading[None, :],
            dense,
            left,
            right,
            admissible,
            ranks,
        )

    wide = P(None, ("row", "col"))
    line = P(("row", "col"))
    placed = (
        wide,
        wide,
        line,
        line,
        line,
        P("row", "col"),
        P("col", "row"),
        P("row", "col"),
        P(),
        P(),
    )
    return jax.shard_map(
        on_device, mesh=mesh, in_specs=placed, out_specs=(wide, wide), check_vma=False
    )
```

time: 159 us -> 134 us (0.84)
  Pallas kernels: 153 us -> 129 us
    pallas_call x1, Pallas kernels: 153 us -> 129 us  [on_device(): pl.pallas_call(functools.partial(kernel, rows, cols), out_shape=(jax.Shap...]
where the time goes in v1:
time: 134 us
  Pallas kernels  129 us (96%)
  local copies, waits for them, and re-layouts  4.52 us (3%)
    pallas_call x1, Pallas kernels, on_device(): pl.pallas_call(functools.partial(kernel, rows, cols), out_shape=(jax.Shap...  129 us
    unnamed x2, local copies, waits for them, and re-layouts  4.52 us

profile of v1, /device:TPU:0, one launch (start us, length us, event | category | flops | bytes accessed | tf_op | source)
XLA Modules:
  0.0 134.1 jit_solution(11560095030729480515)
XLA Ops:
  0.6 129.0 %shard_map.113 = (f32[512,512]{1,0:T(8,128)}, f32[512,512]{1,0:T(8,128)}) custom-call(f32[512,512]{1,0:T(8,128)} %shear_hbm.1, f32[512,512]{1,0:T(8,128)} %state_hbm.1, f32[1,512]{1,0:T(1,128)} %bitcast.3, f32[1,512]{1,0:T(1,128)} %bitcast.4, f32[1,512]{1,0:T(1,128)} %bitcast.5, bf16[2048,4096]{1,0:T(8,128)(2,1)} %dense_ref.1, bf16[128,2048]{1,0:T(8,128)(2,1)} %left_ref.1, ...), custom_call_target="tpu_custom_call" | custom-call | tf_op jit(solution)/shard_map/pallas_call | solution.py:464
  129.6 2.3 %copy.14 = f32[512,512]{1,0:T(8,128)} copy(f32[512,512]{1,0:T(8,128)} %get-tuple-element.4) | data formatting | bytes 2097152
  131.9 2.3 %copy.15 = f32[512,512]{1,0:T(8,128)} copy(f32[512,512]{1,0:T(8,128)} %get-tuple-element.5) | data formatting | bytes 2097152

commit v2 on v1

--- a/solution.py
+++ b/solution.py
@@ -37,9 +37,10 @@
     gathered,
     vsend,
     staged,
+    stage,
     partial,
     psend,
-    precv,
+    arrived,
     own,
     shear,
     state,
@@ -66,17 +67,18 @@
     half = rows // 2
     per = rows // cols
     slots = partial.shape[0]
+    stages = stage.shape[0]
     r = lax.axis_index("row")
     c = lax.axis_index("col")
     mine = c * per
     sib = r + 1 - 2 * (r % 2)
-    targets, sources = weights.shape
+    sources, targets = weights.shape
     across = sources // TILE
     build_rows = 256
     builds = targets // build_rows
     build_cols = 512
     low = c < cols // 2
-    middle = (c > 0) & (c < cols - 1)
+    end = (c == 0) | (c == cols - 1)
 
     def scen(q):
         return pl.ds(pl.multiple_of(q * chunk, chunk), chunk)
@@ -101,10 +103,19 @@
             state.at[scen(q), :], state_out.at[scen(q), :], out_sem.at[1, q]
         )
 
-    def dense_in(b):
-        span = pl.ds(pl.multiple_of(b * build_rows, build_rows), build_rows)
+    def build_order(i):
+        if builds % cols:
+            return i
+        each = builds // cols
+        d = jnp.where(low, c + cols - 1 - i // each, c + 1 + i // each) % cols
+        return d * each + i % each
+
+    def dense_in(i):
+        start = pl.multiple_of(build_order(i) * build_rows, build_rows)
         return pltpu.make_async_copy(
-            dense_ref.at[span, :], weights.at[span, :], dense_sem.at[b]
+            dense_ref.at[pl.ds(start, build_rows), :],
+            stage.at[i % stages],
+            dense_sem.at[i],
         )
 
     def group_of(u, g):
@@ -161,12 +172,11 @@
             device_id_type=MESH,
         )
 
-    def rs_copy(u, d, up):
-        to = jnp.where(up, c + 1, c - 1)
-        slot = jnp.where(up | (d < to), d, cols)
+    def rs_copy(u, d, to):
+        slot = jnp.where(to == d, c, cols + d)
         return pltpu.make_async_remote_copy(
             src_ref=psend.at[u, d],
-            dst_ref=precv.at[u, slot],
+            dst_ref=arrived.at[u, slot],
             send_sem=rs_send.at[u],
             recv_sem=rs_recv.at[u, slot],
             device_id=(r, to),
@@ -175,7 +185,7 @@
 
     def rs_arrival(u, slot):
         return pltpu.make_async_copy(
-            precv.at[u, slot], precv.at[u, slot], rs_recv.at[u, slot]
+            arrived.at[u, slot], arrived.at[u, slot], rs_recv.at[u, slot]
         )
 
     inv_a = 1.0 / a_ref[...]
@@ -246,48 +256,54 @@
 
     def multiply(u, i):
         d = jnp.where(low, c + cols - 1 - i, c + 1 + i) % cols
-        part = lax.dot_general(
+        part = jnp.dot(
             gathered[u],
-            weights[pl.ds(pl.multiple_of(d * piece, piece), piece), :],
-            (((1,), (1,)), ((), ())),
+            weights[:, pl.ds(pl.multiple_of(d * piece, piece), piece)],
             preferred_element_type=F32,
         )
+        held = ((c == 1) & (d > c)) | ((c == cols - 2) & (d < c))
 
         @pl.when(d == c)
         def _():
             own[u % slots] = part
 
-        @pl.when((d != c) & middle)
+        @pl.when(held)
         def _():
             partial[u % slots, d] = part
 
-        @pl.when((d != c) & jnp.logical_not(middle))
+        @pl.when((d != c) & jnp.logical_not(held))
         def _():
             psend[u, d] = part.astype(BF16)
-            rs_copy(u, d, c == 0).start()
-
-    def hop(u, up):
-        def one(i, _):
-            d = jnp.where(up, cols - 1 - i, i)
-            rs_arrival(u, d).wait()
-            psend[u, d] = (partial[u % slots, d] + precv[u, d].astype(F32)).astype(BF16)
-            rs_copy(u, d, up).start()
-            return 0
-
-        @pl.when(middle)
-        def _():
-            lax.fori_loop(0, jnp.where(up, cols - 1 - c, c), one, 0)
+            inner = jnp.where(c == 0, 1, cols - 2)
+            rs_copy(u, d, jnp.where(end, inner, d)).start()
+
+    def hop(u):
+        def one(i, _):
+            d = jnp.where(c == 1, cols - 1 - i, i)
+            rs_arrival(u, cols + d).wait()
+            both = partial[u % slots, d] + arrived[u, cols + d].astype(F32)
+            psend[u, d] = both.astype(BF16)
+            rs_copy(u, d, d).start()
+            return 0
+
+        @pl.when((c == 1) | (c == cols - 2))
+        def _():
+            lax.fori_loop(0, cols - 2, one, 0)
 
     def finish(u):
-        @pl.when(c > 0)
-        def _():
-            rs_arrival(u, c).wait()
-            own[u % slots] = own[u % slots] + precv[u, c].astype(F32)
-
-        @pl.when(c < cols - 1)
-        def _():
-            rs_arrival(u, cols).wait()
-            own[u % slots] = own[u % slots] + precv[u, cols].astype(F32)
+        def one(i, _):
+            s = (c + 1 + i) % cols
+            inner = (s > 0) & (s < cols - 1)
+            beside = ((s == 0) & (c == 1)) | ((s == cols - 1) & (c == cols - 2))
+
+            @pl.when(inner | beside)
+            def _():
+                rs_arrival(u, s).wait()
+                own[u % slots] = own[u % slots] + arrived[u, s].astype(F32)
+
+            return 0
+
+        lax.fori_loop(0, cols - 1, one, 0)
 
         @pl.when(u < chunks)
         def _():
@@ -309,17 +325,11 @@
             shear[here, :] = shear[here, :] + 0.25 * (k_shear[here, :] + ks)
             shear_store(u - chunks).start()
 
-    def build_order(i):
-        if builds % cols:
-            return i
-        each = builds // cols
-        d = jnp.where(low, c + cols - 1 - i // each, c + 1 + i // each) % cols
-        return d * each + i % each
-
     def build(i, _):
         b = build_order(i)
-        dense_in(b).wait()
-        here = pl.ds(pl.multiple_of(b * build_rows, build_rows), build_rows)
+        dense_in(i).wait()
+        start = pl.multiple_of(b * build_rows, build_rows)
+        here = pl.ds(start, build_rows)
         down = targets // TILE
         td = (b * build_rows) // TILE
         for k in range(across):
@@ -328,15 +338,22 @@
             kept = jnp.where(dense == 1, 0, rank)
             left = left_ref[k * RANK : (k + 1) * RANK, here]
             keep = lax.broadcasted_iota(jnp.int32, (RANK, build_rows), 0) < kept
-            left = jnp.where(keep, left.astype(F32), 0.0)
-            left = jnp.transpose(left).astype(BF16)
+            left = jnp.where(keep, left.astype(F32), 0.0).astype(BF16)
             scale = jnp.where(dense == 1, 1.0, 0.0).astype(F32)
-            scale = jnp.full((build_rows, build_cols), scale, F32).astype(BF16)
+            scale = jnp.full((build_cols, build_rows), scale, F32).astype(BF16)
             for s in range(TILE // build_cols):
                 span = slice(k * TILE + s * build_cols, k * TILE + (s + 1) * build_cols)
                 right = right_ref[pl.ds(pl.multiple_of(td * RANK, RANK), RANK), span]
-                term = jnp.dot(left, right, preferred_element_type=F32).astype(BF16)
-                weights[here, span] = weights[here, span] * scale + term
+                term = lax.dot_general(
+                    right, left, (((0,), (0,)), ((), ())), preferred_element_type=F32
+                )
+                turned = jnp.transpose(stage[i % stages, :, span])
+                weights[span, here] = turned * scale + term.astype(BF16)
+
+        @pl.when(i + stages < builds)
+        def _():
+            dense_in(i + stages).start()
+
         return 0
 
     def drain(u):
@@ -374,13 +391,18 @@
     lax.fori_loop(0, chunks, fetch, 0)
 
     def fetch_dense(i, _):
-        dense_in(build_order(i)).start()
-        return 0
-
-    lax.fori_loop(0, builds, fetch_dense, 0)
+        dense_in(i).start()
+        return 0
+
+    lax.fori_loop(0, min(stages, builds), fetch_dense, 0)
     lax.fori_loop(0, chunks, first_slip, 0)
-    cuts = [builds * k // 8 for k in (0, 2, 4, 6, 8)]
-    lax.fori_loop(cuts[0], cuts[1], build, 0)
+    parts = max(8, chunks + 4)
+    cuts = [builds * k // parts for k in range(parts + 1)]
+
+    def build_to(k, n):
+        lax.fori_loop(cuts[k], cuts[k + n], build, 0)
+
+    build_to(0, 2)
     pl.semaphore_wait(barrier, rows + cols - 2)
 
     def first_send(q, _):
@@ -388,17 +410,16 @@
         return 0
 
     lax.fori_loop(0, chunks, first_send, 0)
-    lax.fori_loop(cuts[1], cuts[2], build, 0)
-
-    def first_relay(q, _):
+    build_to(2, 2)
+    done = 4
+    for q in range(chunks):
         relay(q)
-        return 0
-
-    lax.fori_loop(0, chunks, first_relay, 0)
-    lax.fori_loop(cuts[2], cuts[3], build, 0)
-    spread(0)
+        if q == chunks - 2:
+            spread(0)
+        build_to(done, 1)
+        done += 1
     spread(1)
-    lax.fori_loop(cuts[3], cuts[4], build, 0)
+    build_to(done, parts - done)
     forward(0)
 
     gap = max(0, LAG - chunks)
@@ -413,24 +434,22 @@
             body(jnp.where(sigma < chunks, sigma, sigma - gap))
 
     def step(t, _):
-        at_slot(t - 1, lambda u: hop(u, low))
-        early = t + 2 < chunks
-        at_slot(jnp.where(early, t + 2, t + 1), spread, early | (t + 1 >= chunks))
-        at_slot(t - 2, finish)
         at_slot(t, gather_end)
 
         def one(i, _):
             at_slot(t, lambda u: multiply(u, i))
-            at_slot(t + 2, relay, (i == 0) & (t + 2 >= chunks))
-            at_slot(t - 1, lambda u: hop(u, jnp.logical_not(low)), i == 1)
             return 0
 
         lax.fori_loop(0, cols, one, 0)
         at_slot(t + 1, forward)
-        at_slot(t - 4, drain)
-        return 0
-
-    lax.fori_loop(0, units + gap + 2, step, 0)
+        at_slot(t - 1, finish)
+        at_slot(t + 2, spread)
+        at_slot(t, hop)
+        at_slot(t + 3, relay, t + 3 >= chunks)
+        at_slot(t - 3, drain)
+        return 0
+
+    lax.fori_loop(0, units + gap + 1, step, 0)
 
     def last(u, _):
         drain(u)
@@ -456,7 +475,8 @@
         chunk = rows * GROUP
         chunks = scenarios // chunk
         units = 2 * chunks
-        slots = min(units, 4)
+        slots = min(units, 3)
+        stages = 6
         vmem = pl.BlockSpec(memory_space=pltpu.VMEM)
         smem = pl.BlockSpec(memory_space=pltpu.SMEM)
         hbm = pl.BlockSpec(memory_space=pl.ANY)
@@ -470,13 +490,14 @@
             in_specs=[hbm] * 2 + [vmem] * 3 + [hbm, vmem, vmem, smem, smem],
             out_specs=(hbm, hbm),
             scratch_shapes=[
-                pltpu.VMEM(dense.shape, BF16),
+                pltpu.VMEM(dense.shape[::-1], BF16),
                 pltpu.VMEM((units, chunk, dense.shape[1]), BF16),
                 pltpu.VMEM((units, chunk, piece), BF16),
                 pltpu.VMEM((units, rows, GROUP, piece), BF16),
+                pltpu.VMEM((stages, 256, dense.shape[1]), BF16),
                 pltpu.VMEM((slots, cols, chunk, piece), F32),
                 pltpu.VMEM((units, cols, chunk, piece), BF16),
-                pltpu.VMEM((units, cols + 1, chunk, piece), BF16),
+                pltpu.VMEM((units, 2 * cols, chunk, piece), BF16),
                 pltpu.VMEM((slots, chunk, piece), F32),
                 pltpu.VMEM(shear.shape, F32),
                 pltpu.VMEM(shear.shape, F32),
@@ -494,7 +515,7 @@
                 dma((units,)),
                 dma((units,)),
                 dma((units,)),
-                dma((units, cols + 1)),
+                dma((units, 2 * cols)),
             ],
             compiler_params=pltpu.CompilerParams(
                 collective_id=0,

time: 134 us -> 115 us (0.86); the launches traced: 134 us -> 113 us
  Pallas kernels: 129 us -> 108 us
    pallas_call x1, Pallas kernels: 129 us -> 108 us  [on_device(): pl.pallas_call(functools.partial(kernel, rows, cols), out_shape=(jax.Shap...]
where the time goes in v2:
time: 115 us; the launch traced here: 113 us
  Pallas kernels  108 us (94%)
  local copies, waits for them, and re-layouts  4.52 us (4%)
    pallas_call x1, Pallas kernels, on_device(): pl.pallas_call(functools.partial(kernel, rows, cols), out_shape=(jax.Shap...  108 us
    unnamed x2, local copies, waits for them, and re-layouts  4.52 us

profile of v2, /device:TPU:0, one launch (start us, length us, event | category | flops | bytes accessed | tf_op | source)
XLA Modules:
  0.0 113.3 jit_solution(8332342777844287847)
XLA Ops:
  0.6 108.1 %shard_map.113 = (f32[512,512]{1,0:T(8,128)}, f32[512,512]{1,0:T(8,128)}) custom-call(f32[512,512]{1,0:T(8,128)} %shear_hbm.1, f32[512,512]{1,0:T(8,128)} %state_hbm.1, f32[1,512]{1,0:T(1,128)} %bitcast.3, f32[1,512]{1,0:T(1,128)} %bitcast.4, f32[1,512]{1,0:T(1,128)} %bitcast.5, bf16[2048,4096]{1,0:T(8,128)(2,1)} %dense_ref.1, bf16[128,2048]{1,0:T(8,128)(2,1)} %left_ref.1, ...), custom_call_target="tpu_custom_call" | custom-call | tf_op jit(solution)/shard_map/pallas_call | solution.py:484
  108.8 2.3 %copy.14 = f32[512,512]{1,0:T(8,128)} copy(f32[512,512]{1,0:T(8,128)} %get-tuple-element.4) | data formatting | bytes 2097152
  111.0 2.3 %copy.15 = f32[512,512]{1,0:T(8,128)} copy(f32[512,512]{1,0:T(8,128)} %get-tuple-element.5) | data formatting | bytes 2097152

commit v3 on v2

--- a/solution.py
+++ b/solution.py
@@ -27,12 +27,12 @@
     rate_ref,
     load_ref,
     dense_ref,
-    left_ref,
-    right_ref,
+    left_hbm,
+    right_hbm,
     adm_ref,
     rank_ref,
-    shear_out,
-    state_out,
+    shear,
+    state,
     weights,
     gathered,
     vsend,
@@ -42,13 +42,13 @@
     psend,
     arrived,
     own,
-    shear,
-    state,
     k_shear,
     k_state,
+    left_ref,
+    right_ref,
     dense_sem,
+    factor_sem,
     in_sem,
-    out_sem,
     st_send,
     st_recv,
     p1_send,
@@ -78,7 +78,6 @@
     builds = targets // build_rows
     build_cols = 512
     low = c < cols // 2
-    end = (c == 0) | (c == cols - 1)
 
     def scen(q):
         return pl.ds(pl.multiple_of(q * chunk, chunk), chunk)
@@ -91,16 +90,6 @@
     def state_in(q):
         return pltpu.make_async_copy(
             state_hbm.at[scen(q), :], state.at[scen(q), :], in_sem.at[1, q]
-        )
-
-    def shear_store(q):
-        return pltpu.make_async_copy(
-            shear.at[scen(q), :], shear_out.at[scen(q), :], out_sem.at[0, q]
-        )
-
-    def state_store(q):
-        return pltpu.make_async_copy(
-            state.at[scen(q), :], state_out.at[scen(q), :], out_sem.at[1, q]
         )
 
     def build_order(i):
@@ -167,16 +156,16 @@
             src_ref=group_of(u, g),
             dst_ref=group_of(u, g),
             send_sem=sib_send.at[u],
-            recv_sem=sib_recv.at[u],
+            recv_sem=sib_recv.at[u, g // 2],
             device_id=(sib, c),
             device_id_type=MESH,
         )
 
-    def rs_copy(u, d, to):
+    def rs_copy(u, d, to, span):
         slot = jnp.where(to == d, c, cols + d)
         return pltpu.make_async_remote_copy(
-            src_ref=psend.at[u, d],
-            dst_ref=arrived.at[u, slot],
+            src_ref=psend.at[u, d, span],
+            dst_ref=arrived.at[u, slot, span],
             send_sem=rs_send.at[u],
             recv_sem=rs_recv.at[u, slot],
             device_id=(r, to),
@@ -229,35 +218,50 @@
         k_state[scen(q), :] = ks
         return 0
 
+    first_row = (r // half) * half
+
+    def peer(i):
+        inside = half // 2 - 1
+        near = first_row + (r - first_row + 2 * (i + 1)) % half
+        across_rows = (first_row + half) % rows + (r - first_row + 2 * (i - inside)) % half
+        return jnp.where(i < inside, near, across_rows)
+
     def spread(u):
         pltpu.make_async_copy(group_of(u, r), group_of(u, r), p1_recv.at[u]).wait()
 
         def one(i, _):
-            plane_copy(u, r, (r + 2 * (i + 1)) % rows).start()
+            plane_copy(u, r, peer(i)).start()
             return 0
 
         lax.fori_loop(0, half - 1, one, 0)
         sib_copy(u, r).start()
 
+    def forward_from(u, first, last):
+        def one(i, _):
+            plane_copy(u, peer(i), sib).wait_recv()
+            sib_copy(u, peer(i)).start()
+            return 0
+
+        lax.fori_loop(first, last, one, 0)
+
     def forward(u):
-        def one(i, _):
-            g = (r + 2 * (i + 1)) % rows
-            plane_copy(u, g, sib).wait_recv()
-            sib_copy(u, g).start()
-            return 0
-
-        lax.fori_loop(0, half - 1, one, 0)
+        forward_from(u, 0, half - 1)
+
+    def arrive(u, first, last):
+        def one(i, _):
+            g = (first_row + 2 * i + sib % 2) % rows
+            sib_copy(u, g).wait_recv()
+            return 0
+
+        lax.fori_loop(first, last, one, 0)
 
     def gather_end(u):
-        span = pl.ds(0, half * GROUP)
-        pltpu.make_async_copy(
-            gathered.at[u, span, :], gathered.at[u, span, :], sib_recv.at[u]
-        ).wait()
-
-    def multiply(u, i):
+        arrive(u, 0, half)
+
+    def multiply(u, i, span=slice(None)):
         d = jnp.where(low, c + cols - 1 - i, c + 1 + i) % cols
         part = jnp.dot(
-            gathered[u],
+            gathered[u, span],
             weights[:, pl.ds(pl.multiple_of(d * piece, piece), piece)],
             preferred_element_type=F32,
         )
@@ -265,17 +269,17 @@
 
         @pl.when(d == c)
         def _():
-            own[u % slots] = part
+            own[u % slots, span] = part
 
         @pl.when(held)
         def _():
-            partial[u % slots, d] = part
+            partial[u % slots, d, span] = part
 
         @pl.when((d != c) & jnp.logical_not(held))
         def _():
-            psend[u, d] = part.astype(BF16)
-            inner = jnp.where(c == 0, 1, cols - 2)
-            rs_copy(u, d, jnp.where(end, inner, d)).start()
+            psend[u, d, span] = part.astype(BF16)
+            to = jnp.where(c == 0, 1, jnp.where(c == cols - 1, cols - 2, d))
+            rs_copy(u, d, to, span).start()
 
     def hop(u):
         def one(i, _):
@@ -283,7 +287,7 @@
             rs_arrival(u, cols + d).wait()
             both = partial[u % slots, d] + arrived[u, cols + d].astype(F32)
             psend[u, d] = both.astype(BF16)
-            rs_copy(u, d, d).start()
+            rs_copy(u, d, d, slice(None)).start()
             return 0
 
         @pl.when((c == 1) | (c == cols - 2))
@@ -316,14 +320,12 @@
             vsend[u + chunks] = v.astype(BF16)
             send_slip(u + chunks)
             state[here, :] = old + 0.25 * (k1 + k2)
-            state_store(u).start()
 
         @pl.when(u >= chunks)
         def _():
             here = scen(u - chunks)
             ks = load_ref[...] - own[u % slots]
             shear[here, :] = shear[here, :] + 0.25 * (k_shear[here, :] + ks)
-            shear_store(u - chunks).start()
 
     def build(i, _):
         b = build_order(i)
@@ -389,6 +391,10 @@
         return 0
 
     lax.fori_loop(0, chunks, fetch, 0)
+    left_in = pltpu.make_async_copy(left_hbm, left_ref, factor_sem.at[0])
+    right_in = pltpu.make_async_copy(right_hbm, right_ref, factor_sem.at[1])
+    left_in.start()
+    right_in.start()
 
     def fetch_dense(i, _):
         dense_in(i).start()
@@ -402,6 +408,8 @@
     def build_to(k, n):
         lax.fori_loop(cuts[k], cuts[k + n], build, 0)
 
+    left_in.wait()
+    right_in.wait()
     build_to(0, 2)
     pl.semaphore_wait(barrier, rows + cols - 2)
 
@@ -420,7 +428,34 @@
         done += 1
     spread(1)
     build_to(done, parts - done)
-    forward(0)
+    rows_half = chunk // 2
+
+    def unit_half(row):
+        return pl.ds(pl.multiple_of(row * GROUP, rows_half), rows_half)
+
+    upper = unit_half(first_row)
+    lower = unit_half((first_row + half) % rows)
+    inside = half // 2 - 1
+    forward_from(0, 0, inside)
+    arrive(0, 0, half // 2)
+
+    def first_half(i, _):
+        multiply(0, i, upper)
+
+        @pl.when(i == 0)
+        def _():
+            forward_from(0, inside, half - 2)
+
+        return 0
+
+    def second_half(i, _):
+        multiply(0, i, lower)
+        return 0
+
+    lax.fori_loop(0, cols - 2, first_half, 0)
+    forward_from(0, half - 2, half - 1)
+    arrive(0, half // 2, half)
+    lax.fori_loop(0, cols - 2, second_half, 0)
 
     gap = max(0, LAG - chunks)
 
@@ -434,17 +469,17 @@
             body(jnp.where(sigma < chunks, sigma, sigma - gap))
 
     def step(t, _):
-        at_slot(t, gather_end)
-
-        def one(i, _):
-            at_slot(t, lambda u: multiply(u, i))
-            return 0
-
-        lax.fori_loop(0, cols, one, 0)
+        def one(i, _):
+            at_slot(t, lambda u: multiply(u, i), (t > 0) | (i >= cols - 2))
+            return 0
+
+        lax.fori_loop(1, cols, one, 0)
         at_slot(t + 1, forward)
         at_slot(t - 1, finish)
         at_slot(t + 2, spread)
         at_slot(t, hop)
+        at_slot(t + 1, gather_end)
+        at_slot(t + 1, lambda u: multiply(u, 0))
         at_slot(t + 3, relay, t + 3 >= chunks)
         at_slot(t - 3, drain)
         return 0
@@ -457,12 +492,14 @@
 
     lax.fori_loop(units - 2, units, last, 0)
 
-    def stored(q, _):
-        shear_store(q).wait()
-        state_store(q).wait()
-        return 0
-
-    lax.fori_loop(0, chunks, stored, 0)
+
+def hand_over(shear, state, shear_out, state_out, sem):
+    first = pltpu.make_async_copy(shear, shear_out, sem.at[0])
+    second = pltpu.make_async_copy(state, state_out, sem.at[1])
+    first.start()
+    second.start()
+    first.wait()
+    second.wait()
 
 
 def solution(mesh):
@@ -476,19 +513,17 @@
         chunks = scenarios // chunk
         units = 2 * chunks
         slots = min(units, 3)
-        stages = 6
+        half = rows // 2
+        stages = 4
         vmem = pl.BlockSpec(memory_space=pltpu.VMEM)
         smem = pl.BlockSpec(memory_space=pltpu.SMEM)
         hbm = pl.BlockSpec(memory_space=pl.ANY)
         dma = pltpu.SemaphoreType.DMA
-        return pl.pallas_call(
+        after = pl.pallas_call(
             functools.partial(kernel, rows, cols),
-            out_shape=(
-                jax.ShapeDtypeStruct(shear.shape, F32),
-                jax.ShapeDtypeStruct(shear.shape, F32),
-            ),
-            in_specs=[hbm] * 2 + [vmem] * 3 + [hbm, vmem, vmem, smem, smem],
-            out_specs=(hbm, hbm),
+            out_shape=(pltpu.VMEM(shear.shape, F32), pltpu.VMEM(shear.shape, F32)),
+            in_specs=[hbm] * 2 + [vmem] * 3 + [hbm] * 3 + [smem] * 2,
+            out_specs=(vmem, vmem),
             scratch_shapes=[
                 pltpu.VMEM(dense.shape[::-1], BF16),
                 pltpu.VMEM((units, chunk, dense.shape[1]), BF16),
@@ -501,10 +536,10 @@
                 pltpu.VMEM((slots, chunk, piece), F32),
                 pltpu.VMEM(shear.shape, F32),
                 pltpu.VMEM(shear.shape, F32),
-                pltpu.VMEM(shear.shape, F32),
-                pltpu.VMEM(shear.shape, F32),
+                pltpu.VMEM(left.shape, BF16),
+                pltpu.VMEM(right.shape, BF16),
                 dma((dense.shape[0] // 256,)),
-                dma((2, chunks)),
+                dma((2,)),
                 dma((2, chunks)),
                 dma((units,)),
                 dma((units,)),
@@ -513,14 +548,14 @@
                 dma((units,)),
                 dma((units, rows)),
                 dma((units,)),
-                dma((units,)),
+                dma((units, half)),
                 dma((units,)),
                 dma((units, 2 * cols)),
             ],
             compiler_params=pltpu.CompilerParams(
                 collective_id=0,
                 has_side_effects=True,
-                vmem_limit_bytes=62 * 1024 * 1024,
+                vmem_limit_bytes=57 * 1024 * 1024,
             ),
         )(
             shear,
@@ -534,6 +569,17 @@
             admissible,
             ranks,
         )
+        return pl.pallas_call(
+            hand_over,
+            out_shape=(
+                jax.ShapeDtypeStruct(shear.shape, F32),
+                jax.ShapeDtypeStruct(shear.shape, F32),
+            ),
+            in_specs=[vmem] * 2,
+            out_specs=(hbm, hbm),
+            scratch_shapes=[dma((2,))],
+            compiler_params=pltpu.CompilerParams(vmem_limit_bytes=4 * 1024 * 1024),
+        )(*after)
 
     wide = P(None, ("row", "col"))
     line = P(("row", "col"))

time: 115 us -> 109 us (0.948); the launches traced: 113 us -> 109 us
  local copies, waits for them, and re-layouts: 4.52 us -> 0 us
    unnamed x2 -> x0, local copies, waits for them, and re-layouts: 4.52 us -> none
    pallas_call x1 -> x2, Pallas kernels: 108 us -> 108 us  [the longest x1 107 us: on_device(): pl.pallas_call(functools.partial(kernel, rows, cols), out_shape=(pltpu.VM...]
where the time goes in v3:
time: 109 us
  Pallas kernels  108 us (99%)
    pallas_call x1, Pallas kernels, on_device(): pl.pallas_call(functools.partial(kernel, rows, cols), out_shape=(pltpu.VM...  107 us

profile of v3, /device:TPU:0, one launch (start us, length us, event | category | flops | bytes accessed | tf_op | source)
XLA Modules:
  0.0 108.5 jit_solution(6232644126981012197)
XLA Ops:
  0.6 106.6 %shard_map.113 = (f32[512,512]{1,0:T(8,128)S(1)}, f32[512,512]{1,0:T(8,128)S(1)}) custom-call(f32[512,512]{1,0:T(8,128)} %shear_hbm.1, f32[512,512]{1,0:T(8,128)} %state_hbm.1, f32[1,512]{1,0:T(1,128)} %bitcast.3, f32[1,512]{1,0:T(1,128)} %bitcast.4, f32[1,512]{1,0:T(1,128)} %bitcast.5, bf16[2048,4096]{1,0:T(8,128)(2,1)} %dense_ref.1, ...), custom_call_target="tpu_custom_call" | custom-call | tf_op jit(solution)/shard_map/pallas_call | solution.py:522
  107.2 1.3 %shard_map.114 = (f32[512,512]{1,0:T(8,128)}, f32[512,512]{1,0:T(8,128)}) custom-call(f32[512,512]{1,0:T(8,128)S(1)} %get-tuple-element.4.shear, f32[512,512]{1,0:T(8,128)S(1)} %get-tuple-element.5.state), custom_call_target="tpu_custom_call" | custom-call | tf_op jit(solution)/shard_map/pallas_call | solution.py:572

commit v4 on v3

--- a/solution.py
+++ b/solution.py
@@ -23,14 +23,14 @@
     cols,
     shear_hbm,
     state_hbm,
-    a_ref,
-    rate_ref,
-    load_ref,
+    a_hbm,
+    rate_hbm,
+    load_hbm,
     dense_ref,
     left_hbm,
     right_hbm,
-    adm_ref,
-    rank_ref,
+    adm_hbm,
+    rank_hbm,
     shear,
     state,
     weights,
@@ -46,8 +46,13 @@
     k_state,
     left_ref,
     right_ref,
+    a_ref,
+    rate_ref,
+    load_ref,
+    adm_ref,
+    rank_ref,
     dense_sem,
-    factor_sem,
+    small_sem,
     in_sem,
     st_send,
     st_recv,
@@ -118,7 +123,7 @@
             src_ref=part_of(u, j),
             dst_ref=staged.at[u, r],
             send_sem=st_send.at[u],
-            recv_sem=st_recv.at[u],
+            recv_sem=st_recv.at[u % chunks],
             device_id=(j, c),
             device_id_type=MESH,
         )
@@ -136,7 +141,7 @@
             src_ref=staged.at[u, source],
             dst_ref=place(u, source),
             send_sem=p1_send.at[u],
-            recv_sem=p1_recv.at[u],
+            recv_sem=p1_recv.at[u % chunks],
             device_id=(r, source // per),
             device_id_type=MESH,
         )
@@ -146,7 +151,7 @@
             src_ref=group_of(u, g),
             dst_ref=group_of(u, g),
             send_sem=p2_send.at[u],
-            recv_sem=p2_recv.at[u, g],
+            recv_sem=p2_recv.at[u % chunks, g // 2],
             device_id=(row_to, c),
             device_id_type=MESH,
         )
@@ -156,7 +161,7 @@
             src_ref=group_of(u, g),
             dst_ref=group_of(u, g),
             send_sem=sib_send.at[u],
-            recv_sem=sib_recv.at[u, g // 2],
+            recv_sem=sib_recv.at[u % chunks, g // 2],
             device_id=(sib, c),
             device_id_type=MESH,
         )
@@ -167,20 +172,18 @@
             src_ref=psend.at[u, d, span],
             dst_ref=arrived.at[u, slot, span],
             send_sem=rs_send.at[u],
-            recv_sem=rs_recv.at[u, slot],
+            recv_sem=rs_recv.at[u % chunks, slot],
             device_id=(r, to),
             device_id_type=MESH,
         )
 
     def rs_arrival(u, slot):
         return pltpu.make_async_copy(
-            arrived.at[u, slot], arrived.at[u, slot], rs_recv.at[u, slot]
-        )
-
-    inv_a = 1.0 / a_ref[...]
+            arrived.at[u, slot], arrived.at[u, slot], rs_recv.at[u % chunks, slot]
+        )
 
     def velocity(shear_now, state_now):
-        x = shear_now * inv_a
+        x = shear_now * a_ref[...]
         fade = jnp.exp(-state_now)
         v = (jnp.exp(x - LN2) - jnp.exp(-x - LN2)) * fade
         return v, rate_ref[...] * (fade - jnp.abs(v))
@@ -191,10 +194,10 @@
             return 0
 
         lax.fori_loop(0, rows - 1, one, 0)
-        pltpu.make_async_copy(part_of(u, r), staged.at[u, r], st_recv.at[u]).start()
+        pltpu.make_async_copy(part_of(u, r), staged.at[u, r], st_recv.at[u % chunks]).start()
 
     def relay(u):
-        pltpu.make_async_copy(staged.at[u], staged.at[u], st_recv.at[u]).wait()
+        pltpu.make_async_copy(staged.at[u], staged.at[u], st_recv.at[u % chunks]).wait()
 
         def one(i, _):
             p1_copy(u, (mine + per + i) % rows).start()
@@ -204,7 +207,7 @@
 
         def stay(i, _):
             pltpu.make_async_copy(
-                staged.at[u, mine + i], place(u, mine + i), p1_recv.at[u]
+                staged.at[u, mine + i], place(u, mine + i), p1_recv.at[u % chunks]
             ).start()
             return 0
 
@@ -227,7 +230,7 @@
         return jnp.where(i < inside, near, across_rows)
 
     def spread(u):
-        pltpu.make_async_copy(group_of(u, r), group_of(u, r), p1_recv.at[u]).wait()
+        pltpu.make_async_copy(group_of(u, r), group_of(u, r), p1_recv.at[u % chunks]).wait()
 
         def one(i, _):
             plane_copy(u, r, peer(i)).start()
@@ -385,41 +388,58 @@
     lax.fori_loop(0, rows - 1, greet_row, 0)
     lax.fori_loop(0, cols - 1, greet_col, 0)
 
+    small = [
+        pltpu.make_async_copy(src, dst, small_sem.at[k])
+        for k, (src, dst) in enumerate(
+            (
+                (a_hbm, a_ref),
+                (rate_hbm, rate_ref),
+                (load_hbm, load_ref),
+                (adm_hbm, adm_ref),
+                (rank_hbm, rank_ref),
+                (left_hbm, left_ref),
+                (right_hbm, right_ref),
+            )
+        )
+    ]
+    for copy in small:
+        copy.start()
+
     def fetch(q, _):
         shear_in(q).start()
         state_in(q).start()
         return 0
 
     lax.fori_loop(0, chunks, fetch, 0)
-    left_in = pltpu.make_async_copy(left_hbm, left_ref, factor_sem.at[0])
-    right_in = pltpu.make_async_copy(right_hbm, right_ref, factor_sem.at[1])
-    left_in.start()
-    right_in.start()
 
     def fetch_dense(i, _):
         dense_in(i).start()
         return 0
 
     lax.fori_loop(0, min(stages, builds), fetch_dense, 0)
-    lax.fori_loop(0, chunks, first_slip, 0)
+    for copy in small[:3]:
+        copy.wait()
+    a_ref[...] = 1.0 / a_ref[...]
+    lax.fori_loop(0, 1, first_slip, 0)
     parts = max(8, chunks + 4)
     cuts = [builds * k // parts for k in range(parts + 1)]
 
     def build_to(k, n):
         lax.fori_loop(cuts[k], cuts[k + n], build, 0)
 
-    left_in.wait()
-    right_in.wait()
-    build_to(0, 2)
+    for copy in small[3:]:
+        copy.wait()
     pl.semaphore_wait(barrier, rows + cols - 2)
 
     def first_send(q, _):
         send_slip(q)
         return 0
 
-    lax.fori_loop(0, chunks, first_send, 0)
-    build_to(2, 2)
-    done = 4
+    first_send(0, 0)
+    lax.fori_loop(1, chunks, first_slip, 0)
+    lax.fori_loop(1, chunks, first_send, 0)
+    build_to(0, 2)
+    done = 2
     for q in range(chunks):
         relay(q)
         if q == chunks - 2:
@@ -516,13 +536,12 @@
         half = rows // 2
         stages = 4
         vmem = pl.BlockSpec(memory_space=pltpu.VMEM)
-        smem = pl.BlockSpec(memory_space=pltpu.SMEM)
         hbm = pl.BlockSpec(memory_space=pl.ANY)
         dma = pltpu.SemaphoreType.DMA
         after = pl.pallas_call(
             functools.partial(kernel, rows, cols),
             out_shape=(pltpu.VMEM(shear.shape, F32), pltpu.VMEM(shear.shape, F32)),
-            in_specs=[hbm] * 2 + [vmem] * 3 + [hbm] * 3 + [smem] * 2,
+            in_specs=[hbm] * 10,
             out_specs=(vmem, vmem),
             scratch_shapes=[
                 pltpu.VMEM(dense.shape[::-1], BF16),
@@ -538,19 +557,24 @@
                 pltpu.VMEM(shear.shape, F32),
                 pltpu.VMEM(left.shape, BF16),
                 pltpu.VMEM(right.shape, BF16),
+                pltpu.VMEM((1, piece), F32),
+                pltpu.VMEM((1, piece), F32),
+                pltpu.VMEM((1, piece), F32),
+                pltpu.SMEM(admissible.shape, jnp.int32),
+                pltpu.SMEM(ranks.shape, jnp.int32),
                 dma((dense.shape[0] // 256,)),
-                dma((2,)),
+                dma((7,)),
                 dma((2, chunks)),
                 dma((units,)),
+                dma((chunks,)),
                 dma((units,)),
+                dma((chunks,)),
                 dma((units,)),
+                dma((chunks, half)),
                 dma((units,)),
+                dma((chunks, half)),
                 dma((units,)),
-                dma((units, rows)),
-                dma((units,)),
-                dma((units, half)),
-                dma((units,)),
-                dma((units, 2 * cols)),
+                dma((chunks, 2 * cols)),
             ],
             compiler_params=pltpu.CompilerParams(
                 collective_id=0,

time: 109 us -> 104 us (0.954)
  Pallas kernels: 108 us -> 103 us
    pallas_call x1, Pallas kernels: 107 us -> 102 us  [on_device(): pl.pallas_call(functools.partial(kernel, rows, cols), out_shape=(pltpu.VM...]
where the time goes in v4:
time: 104 us
  Pallas kernels  103 us (99%)
    pallas_call x1, Pallas kernels, on_device(): pl.pallas_call(functools.partial(kernel, rows, cols), out_shape=(pltpu.VM...  102 us

profile of v4, /device:TPU:0, one launch (start us, length us, event | category | flops | bytes accessed | tf_op | source)
XLA Modules:
  0.0 103.5 jit_solution(1685179973625210581)
XLA Ops:
  0.6 101.6 %shard_map.113 = (f32[512,512]{1,0:T(8,128)S(1)}, f32[512,512]{1,0:T(8,128)S(1)}) custom-call(f32[512,512]{1,0:T(8,128)} %shear_hbm.1, f32[512,512]{1,0:T(8,128)} %state_hbm.1, f32[1,512]{1,0:T(1,128)} %bitcast.3, f32[1,512]{1,0:T(1,128)} %bitcast.4, f32[1,512]{1,0:T(1,128)} %bitcast.5, bf16[2048,4096]{1,0:T(8,128)(2,1)} %dense_ref.1, ...), custom_call_target="tpu_custom_call" | custom-call | tf_op jit(solution)/shard_map/pallas_call | solution.py:541
  102.2 1.3 %shard_map.114 = (f32[512,512]{1,0:T(8,128)}, f32[512,512]{1,0:T(8,128)}) custom-call(f32[512,512]{1,0:T(8,128)S(1)} %get-tuple-element.4.shear, f32[512,512]{1,0:T(8,128)S(1)} %get-tuple-element.5.state), custom_call_target="tpu_custom_call" | custom-call | tf_op jit(solution)/shard_map/pallas_call | solution.py:596
